TPU v7x, 32 devices: a whole 2x2x4 slice. The times are simulated.
32 devices in a mesh: tm: 8 (over y, x, core), mp: 4 (over z).
Axes of the slice: x: 2, y: 2, z: 4, core: 2. Of those that a mesh axis runs over, the one named last changes fastest.
Arguments:
- frames: bfloat16 [4096, 1024], P(('tm', 'mp')), may hold values from -6 to 6
- block_ids: int32 [4096], replicated, may hold values from 0 to 203, never falling along the last dimension, each value on 1 to 40 neighbouring positions
- valid_counts: int32 [8], replicated, may hold values from 1 to 512, as said below
- norm_attn: float32 [1024], replicated, may hold values from 0.25 to 1.75
- w_qkv: bfloat16 [1024, 3072], replicated, may hold values from -1 to 1
- w_attn_out: bfloat16 [1024, 1024], replicated, may hold values from -0.1875 to 0.1875
- norm_conv: float32 [1024], replicated, may hold values from 0.25 to 1.75
- w_point_in: bfloat16 [1024, 2048], replicated, may hold values from -0.1875 to 0.1875
- w_depth: bfloat16 [31, 1024], replicated, may hold values from -1 to 1
- w_point_out: bfloat16 [1024, 1024], replicated, may hold values from -0.1875 to 0.1875
- w_adapter: bfloat16 [1024, 8192], P('tm', 'mp'), may hold values from -1 to 1
- llm_gain: float32 [8192], replicated, may hold values from 0.25 to 1.75
- w_query: bfloat16 [8192, 8192], P('tm', 'mp'), may hold values from -1 to 1
- w_key: bfloat16 [8192, 1024], P('tm', 'mp'), may hold values from -1 to 1
- w_value: bfloat16 [8192, 1024], P('tm', 'mp'), may hold values from -0.0625 to 0.0625
Outputs:
- conf_out: bfloat16 [4096, 1024], P(('tm', 'mp'))
- attended: bfloat16 [1024, 8192], P('tm', 'mp')
Inputs may be any that keep to these rules, and one draw needn't show every extreme that they name: `block_ids`: block numbers never fall along the recording, and one block holds 1 to 40 frames. Every time shard but the last holds 512 real frames; the frames after the first valid_counts[t] of time shard t are padding.
All inputs are finite; a program needn't handle non-finite values.
Results may differ from a plain program's by a relative error of at most 0.014.
Values may be sent and summed in bfloat16 or wider, within the bound.
No kernel may reach another device: no remote copies, remote signals or barrier semaphores. Data moves between devices by JAX's collectives and lax.ppermute only.
A program may use at most 192 MiB of HBM per device.

v0:
```python
import math
import jax
import jax.numpy as jnp
from jax import lax
from jax.sharding import PartitionSpec as P

CH = 16
HDIM = 128
eps_conf = 1e-05
eps_llm = 1e-06
rope_base = 1000000.0
masked_score = -1e30


def passed_along(value, axis, by):
    length = lax.axis_size(axis)
    pairs = [(i, i + by) for i in range(length) if 0 <= i + by < length]
    return lax.ppermute(value, axis, pairs)


def shard_count(index, valid_counts, shard_len):
    shard = index // shard_len
    table = jnp.arange(valid_counts.shape[0], dtype=jnp.int32)
    hit = shard[:, None] == table[None, :]
    count = jnp.sum(jnp.where(hit, valid_counts[None, :], 0), axis=1)
    return (index - shard * shard_len, count)


def layer_norm(field, gain):
    center = field - jnp.mean(field, axis=-1, keepdims=True)
    spread = jnp.mean(center * center, axis=-1, keepdims=True)
    return center * lax.rsqrt(spread + eps_conf) * gain


def rotary(field, positions):
    half = field.shape[-1] // 2
    freq = rope_base ** (-(jnp.arange(half, dtype=jnp.float32) * 2.0) / field.shape[-1])
    angle = positions.astype(jnp.float32)[:, None] * freq[None, :]
    cosine = jnp.concatenate([jnp.cos(angle), jnp.cos(angle)], axis=-1)[:, None, :]
    sine = jnp.concatenate([jnp.sin(angle), jnp.sin(angle)], axis=-1)[:, None, :]
    turned = jnp.concatenate([-field[..., half:], field[..., :half]], axis=-1)
    return field * cosine + turned * sine


def on_device(
    frames,
    block_ids,
    valid_counts,
    norm_attn,
    w_qkv,
    w_attn_out,
    norm_conv,
    w_point_in,
    w_depth,
    w_point_out,
    w_adapter,
    llm_gain,
    w_query,
    w_key,
    w_value,
):
    mp_count = lax.axis_size("mp")
    frame_rows, width = frames.shape
    heads = CH
    head_size = width // heads
    shard_frames = frame_rows * mp_count
    time_place = lax.axis_index("tm")
    model_place = lax.axis_index("mp")
    first = (time_place * mp_count + model_place) * frame_rows
    inputs = frames.astype(jnp.float32)
    own_index = first + jnp.arange(frame_rows, dtype=jnp.int32)
    own_place, own_count = shard_count(own_index, valid_counts, shard_frames)
    frame_real = own_place < own_count
    normed = layer_norm(inputs, norm_attn).astype(jnp.bfloat16)
    projected = jnp.dot(normed, w_qkv, preferred_element_type=jnp.float32).astype(jnp.bfloat16)
    queries = projected[:, :width]
    own_keys = projected[:, width : 2 * width]
    own_values = projected[:, 2 * width :]
    prior_keys, prior_values = passed_along((own_keys, own_values), ("tm", "mp"), 1)
    keys = jnp.concatenate([prior_keys, own_keys], axis=0).reshape(2 * frame_rows, heads, head_size)
    values = jnp.concatenate([prior_values, own_values], axis=0).reshape(
        2 * frame_rows, heads, head_size
    )
    key_index = first - frame_rows + jnp.arange(2 * frame_rows, dtype=jnp.int32)
    key_place, key_count = shard_count(key_index, valid_counts, shard_frames)
    key_real = key_place < key_count
    prior_ids = lax.dynamic_slice_in_dim(
        block_ids, jnp.maximum(first - frame_rows, 0), frame_rows, 0
    )
    query_ids = lax.dynamic_slice_in_dim(block_ids, first, frame_rows, 0)
    key_ids = jnp.concatenate([prior_ids, query_ids], axis=0)
    same = key_index[None, :] == own_index[:, None]
    visible = (
        (key_index[None, :] <= own_index[:, None])
        & (key_ids[None, :] >= query_ids[:, None] - 2)
        & (key_real[None, :] | same)
    )
    query_heads = queries.reshape(frame_rows, heads, head_size)
    scores = jnp.einsum(
        "qhd,khd->hqk", query_heads, keys, preferred_element_type=jnp.float32
    ) / jnp.sqrt(jnp.float32(head_size))
    scores = jnp.where(visible[None], scores, masked_score)
    top = jnp.max(scores, axis=-1, keepdims=True)
    weights = jnp.where(visible[None], jnp.exp(scores - top), 0.0)
    total = jnp.sum(weights, axis=-1)
    summed = jnp.einsum(
        "hqk,khd->qhd", weights.astype(jnp.bfloat16), values, preferred_element_type=jnp.float32
    )
    conf_context = (
        (summed / jnp.transpose(total)[:, :, None]).reshape(frame_rows, width).astype(jnp.bfloat16)
    )
    mid = inputs + jnp.dot(conf_context, w_attn_out, preferred_element_type=jnp.float32)
    conv_in = layer_norm(mid, norm_conv).astype(jnp.bfloat16)
    both = jnp.dot(conv_in, w_point_in, preferred_element_type=jnp.float32)
    glu = both[:, :width] * jax.nn.sigmoid(both[:, width:])
    glu = jnp.where(frame_real[:, None], glu, 0.0).astype(jnp.bfloat16)
    taps = w_depth.shape[0]
    rim = passed_along(glu[frame_rows - (taps - 1) :], ("tm", "mp"), 1)
    padded = jnp.concatenate([rim, glu], axis=0).astype(jnp.float32)
    kernel = w_depth.astype(jnp.float32)
    depth = jnp.zeros((frame_rows, width), jnp.float32)
    for tap in range(taps):
        depth = depth + kernel[tap][None, :] * padded[taps - 1 - tap : taps - 1 - tap + frame_rows]
    activated = jax.nn.silu(depth).astype(jnp.bfloat16)
    final = mid + jnp.dot(activated, w_point_out, preferred_element_type=jnp.float32)
    conf_out = jnp.where(frame_real[:, None], final, 0.0).astype(jnp.bfloat16)
    pooled = (
        jnp.sum(conf_out.astype(jnp.float32).reshape(frame_rows // 4, 4, width), axis=1) * 0.25
    ).astype(jnp.bfloat16)
    shard_pooled = lax.all_gather(pooled, "mp", axis=0, tiled=True)
    shard_tokens = shard_pooled.shape[0]
    adapter_part = lax.all_gather(w_adapter, "tm", axis=0, tiled=True)
    adapter_full = lax.all_gather(adapter_part, "mp", axis=1, tiled=True)
    adapted = jnp.dot(shard_pooled, adapter_full, preferred_element_type=jnp.float32)
    llm_in = (
        adapted
        * lax.rsqrt(jnp.mean(adapted * adapted, axis=-1, keepdims=True) + eps_llm)
        * llm_gain
    ).astype(jnp.bfloat16)
    query_cols = w_query.shape[1]
    key_cols = w_key.shape[1]
    raw_query = jnp.dot(
        llm_in,
        lax.all_gather(w_query, "tm", axis=0, tiled=True),
        preferred_element_type=jnp.float32,
    )
    raw_keys = jnp.dot(
        llm_in, lax.all_gather(w_key, "tm", axis=0, tiled=True), preferred_element_type=jnp.float32
    )
    raw_values = jnp.dot(
        llm_in,
        lax.all_gather(w_value, "tm", axis=0, tiled=True),
        preferred_element_type=jnp.float32,
    )
    llm_size = HDIM
    query_heads_dev = query_cols // llm_size
    kv_heads = key_cols // llm_size
    group = query_heads_dev // kv_heads
    token_index = time_place * shard_tokens + jnp.arange(shard_tokens, dtype=jnp.int32)
    llm_query = rotary(
        raw_query.reshape(shard_tokens, query_heads_dev, llm_size), token_index
    ).astype(jnp.bfloat16)
    llm_query = llm_query.reshape(shard_tokens, kv_heads, group, llm_size)
    llm_keys = (
        rotary(raw_keys.reshape(shard_tokens, kv_heads, llm_size), token_index)
        .astype(jnp.bfloat16)
        .reshape(shard_tokens, key_cols)
    )
    llm_values = raw_values.astype(jnp.bfloat16)
    score_scale = 1.0 / jnp.sqrt(jnp.float32(llm_size))
    start_state = (
        jnp.full((kv_heads, group, shard_tokens), masked_score, jnp.float32),
        jnp.zeros((kv_heads, group, shard_tokens), jnp.float32),
        jnp.zeros((kv_heads, group, shard_tokens, llm_size), jnp.float32),
    )
    key_piece = lax.all_gather(llm_keys, "tm", axis=0, tiled=True)
    value_piece = lax.all_gather(llm_values, "tm", axis=0, tiled=True)
    piece_rows = key_piece.shape[0]
    step_rows = math.gcd(piece_rows, 512)

    def one_step(block, state):
        best, total_weight, accum = state
        key_block = lax.dynamic_slice_in_dim(key_piece, block * step_rows, step_rows, 0).reshape(
            step_rows, kv_heads, llm_size
        )
        value_block = lax.dynamic_slice_in_dim(
            value_piece, block * step_rows, step_rows, 0
        ).reshape(step_rows, kv_heads, llm_size)
        block_index = block * step_rows + jnp.arange(step_rows, dtype=jnp.int32)
        block_place, block_count = shard_count(block_index, valid_counts, shard_tokens)
        block_real = block_place * 4 < block_count
        matches = block_index[None, :] == token_index[:, None]
        seen = (block_index[None, :] <= token_index[:, None]) & (block_real[None, :] | matches)
        block_scores = (
            jnp.einsum("qhgd,khd->hgqk", llm_query, key_block, preferred_element_type=jnp.float32)
            * score_scale
        )
        block_scores = jnp.where(seen[None, None], block_scores, masked_score)
        new_best = jnp.maximum(best, jnp.max(block_scores, axis=-1))
        block_weights = jnp.where(
            seen[None, None], jnp.exp(block_scores - new_best[..., None]), 0.0
        )
        fade = jnp.exp(best - new_best)
        total_weight = total_weight * fade + jnp.sum(block_weights, axis=-1)
        accum = accum * fade[..., None] + jnp.einsum(
            "hgqk,khd->hgqd",
            block_weights.astype(jnp.bfloat16),
            value_block,
            preferred_element_type=jnp.float32,
        )
        return (new_best, total_weight, accum)

    best, total_weight, accum = lax.fori_loop(0, piece_rows // step_rows, one_step, start_state)
    result = accum / total_weight[..., None]
    attended = (
        jnp.transpose(result, (2, 0, 1, 3)).reshape(shard_tokens, query_cols).astype(jnp.bfloat16)
    )
    return (conf_out, attended)


def solution(mesh):
    placed = (
        P(("tm", "mp"), None),
        P(),
        P(),
        P(),
        P(),
        P(),
        P(),
        P(),
        P(),
        P(),
        P("tm", "mp"),
        P(),
        P("tm", "mp"),
        P("tm", "mp"),
        P("tm", "mp"),
    )
    return jax.shard_map(
        on_device,
        mesh=mesh,
        in_specs=placed,
        out_specs=(P(("tm", "mp"), None), P("tm", "mp")),
        check_vma=False,
    )
```

profile of v0, /device:TPU:0, one launch (start us, length us, event | category | flops | bytes accessed | tf_op | source)
XLA Modules:
  0.0 644.8 jit_solution(2328061743884182033)
XLA Ops:
  8.0 41.4 %all-gather.6.cloned.1.call-done = bf16[1024,2048]{1,0:T(8,128)(2,1)} async-done(((bf16[128,2048]{1,0:T(8,128)(2,1)}), bf16[1024,2048]{1,0:T(8,128)(2,1)}) %all-gather.6.cloned.1.call-update) | async-done | bytes 4194320 | tf_op jit(solution)/shard_map/all_gather | solution.py:132
  51.7 3.9 convolution_convert_fusion
  56.3 3.4 collective-permute-start.1
  59.7 4.1 collective-permute-start
  69.6 10.4 %collective-permute-done = bf16[128,1024]{1,0:T(8,128)(2,1)} collective-permute-done((bf16[128,1024]{1,0:T(8,128)(2,1)}, bf16[128,1024]{1,0:T(8,128)(2,1)}, u32[]{:S(2)}, u32[]{:S(2)}) %collective-permute-start) | collective-permute-done | bytes 262176 | tf_op jit(solution)/shard_map/ppermute | solution.py:18
  82.1 2.0 fusion.95
  86.0 3.9 fusion.22
  91.0 3.1 fusion.72
  94.3 13.2 %collective-permute-start.2 = (bf16[30,1024]{1,0:T(8,128)(2,1)S(1)}, bf16[30,1024]{1,0:T(8,128)(2,1)S(1)}, u32[]{:S(2)}, u32[]{:S(2)}) collective-permute-start(bf16[30,1024]{1,0:T(8,128)(2,1)S(1)} %slice.294), channel_id=1, source_target_pairs={{0,1},{1,2},{2,3},{3,4},{4,5},{5,6},{6,7},{7,8},{8,9},{9,10},{10,1... | collective-permute-start | bytes 184328 | tf_op jit(solution)/shard_map/ppermute | solution.py:18
  107.6 3.0 collective-permute-done.2
  111.1 2.5 fusion.23
  114.1 36.5 %all_gather.24 = bf16[128,1024]{1,0:T(8,128)(2,1)S(1)} all-gather(bf16[32,1024]{1,0:T(8,128)(2,1)S(1)} %multiply_convert_fusion.5), channel_id=1, replica_groups=mesh['tm'=8,'mp'=4] {'mp'}, dimensions={0}, use_global_device_ids=true | all-gather | bytes 327680 | tf_op jit(solution)/shard_map/all_gather | solution.py:130
  150.6 200.2 %all-gather.8.cloned.1.call-done = bf16[1024,8192]{1,0:T(8,128)(2,1)} async-done(((bf16[1024,2048]{1,0:T(8,128)(2,1)}), bf16[1024,8192]{1,0:T(8,128)(2,1)}) %all-gather.8.cloned.1.call-update) | async-done | bytes 16777232 | tf_op jit(solution)/shard_map/all_gather | solution.py:133
  350.8 8.2 %multiply_reduce_fusion = (f32[128]{0:T(128)S(1)}, f32[128,8192]{1,0:T(8,128)S(1)}) fusion(bf16[128,1024]{1,0:T(8,128)(2,1)S(1)} %all_gather.24, bf16[1024,8192]{1,0:T(8,128)(2,1)} %all-gather.8.cloned.1.call-done), kind=kOutput, calls=%fused_computation.35 | convolution fusion | flops 2149580800 | bytes 21234176 | tf_op jit(solution)/shard_map/dot_general | solution.py:134
  359.5 27.4 %all-gather.10.cloned.1.call-done = bf16[8192,256]{1,0:T(8,128)(2,1)} async-done(((bf16[1024,256]{1,0:T(8,128)(2,1)}), bf16[8192,256]{1,0:T(8,128)(2,1)}) %all-gather.10.cloned.1.call-update) | async-done | bytes 4194320 | tf_op jit(solution)/shard_map/all_gather | solution.py:148
  386.9 2.9 fusion.98
  390.4 12.2 %all_gather.28 = bf16[1024,256]{1,0:T(8,128)(2,1)} all-gather(bf16[128,256]{1,0:T(8,128)(2,1)S(1)} %fusion.82), channel_id=1, replica_groups=mesh['tm'=8,'mp'=4] {'tm'}, dimensions={0}, use_global_device_ids=true | all-gather | bytes 589824 | tf_op jit(solution)/shard_map/all_gather | solution.py:176
  402.6 23.5 %all-gather.14.cloned.1.call-done = bf16[8192,256]{1,0:T(8,128)(2,1)} async-done(((bf16[1024,256]{1,0:T(8,128)(2,1)}), bf16[8192,256]{1,0:T(8,128)(2,1)}) %all-gather.14.cloned.1.call-update) | async-done | bytes 4194320 | tf_op jit(solution)/shard_map/all_gather | solution.py:152
  426.1 2.9 convolution_convert_fusion.1
  429.0 10.8 %all_gather.31 = bf16[1024,256]{1,0:T(8,128)(2,1)} all-gather(bf16[128,256]{1,0:T(8,128)(2,1)S(1)} %convolution_convert_fusion.1), channel_id=1, replica_groups=mesh['tm'=8,'mp'=4] {'tm'}, dimensions={0}, use_global_device_ids=true | all-gather | bytes 589824 | tf_op jit(solution)/shard_map/all_gather | solution.py:177
  439.8 148.9 %all-gather.12.cloned.1.call-done = bf16[8192,2048]{1,0:T(8,128)(2,1)} async-done(((bf16[1024,2048]{1,0:T(8,128)(2,1)}), bf16[8192,2048]{1,0:T(8,128)(2,1)}) %all-gather.12.cloned.1.call-update) | async-done | bytes 33554448 | tf_op jit(solution)/shard_map/all_gather | solution.py:144
  588.7 12.9 %fusion.99 = f32[128,2048]{1,0:T(8,128)S(1)} fusion(bf16[128,8192]{1,0:T(8,128)(2,1)S(1)} %multiply_convert_fusion, bf16[8192,2048]{1,0:T(8,128)(2,1)} %all-gather.12.cloned.1.call-done), kind=kOutput, calls=%fused_computation.199 | convolution fusion | flops 4294967296 | bytes 36700160 | tf_op jit(solution)/shard_map/dot_general | solution.py:142
  603.0 2.4 copy.57
  605.4 2.4 copy.58
  608.0 2.2 fusion.25
  610.2 25.0 %while.20 = (s32[]{:T(128)}, f32[2,8,128]{2,1,0:T(8,128)S(1)}, f32[2,8,128]{2,1,0:T(8,128)S(1)}, f32[2,8,128,128]{3,2,1,0:T(8,128)}, s32[8]{0:T(128)S(1)}, /*ind...) while((s32[]{:T(128)}, f32[2,8,128]{2,1,0:T(8,128)S(1)}, ...), condition=%wide.region_14.15_spmd.clone, body=%wide.region_10.14_spmd.clone.sunk | while | flops 551591552 | bytes 26622240 | solution.py:213
  611.7 2.8 fusion.133
  614.6 3.2 fusion.134
  617.9 3.9 fusion.136
  624.3 2.8 fusion.133
  627.1 3.2 fusion.134
  630.4 3.9 fusion.136
  (184 shorter events, 26.0 us)
Async XLA Ops:
  7.2 82.7 %copy-start = (bf16[1024,1024]{1,0:T(8,128)(2,1)S(1)}, bf16[1024,1024]{1,0:T(8,128)(2,1)}, u32[]{:S(2)}) copy-start(bf16[1024,1024]{1,0:T(8,128)(2,1)} %param.22) | copy-start | bytes 6291460
  7.2 42.2 %all-gather.6.cloned.1.call-start = ((), (), s32[]{:S(2)}) async-start(), calls=%async_computation | async-start | bytes 4718592 | tf_op jit(solution)/shard_map/all_gather | solution.py:132
  7.9 342.8 %all-gather.8.cloned.1.call-start = ((), (), s32[]{:S(2)}) async-start(), calls=%async_computation.1 | async-start | bytes 20971520 | tf_op jit(solution)/shard_map/all_gather | solution.py:133
  49.4 337.5 %all-gather.10.cloned.1.call-start = ((), (), s32[]{:S(2)}) async-start(), calls=%async_computation.2 | async-start | bytes 4718592 | tf_op jit(solution)/shard_map/all_gather | solution.py:148
  50.1 376.0 %all-gather.14.cloned.1.call-start = ((), (), s32[]{:S(2)}) async-start(), calls=%async_computation.4 | async-start | bytes 4718592 | tf_op jit(solution)/shard_map/all_gather | solution.py:152
  50.7 538.0 %all-gather.12.cloned.1.call-start = ((), (), s32[]{:S(2)}) async-start(), calls=%async_computation.3 | async-start | bytes 37748736 | tf_op jit(solution)/shard_map/all_gather | solution.py:144
  56.3 13.0 %collective-permute-start.1 = (bf16[128,1024]{1,0:T(8,128)(2,1)S(1)}, bf16[128,1024]{1,0:T(8,128)(2,1)S(1)}, u32[]{:S(2)}, u32[]{:S(2)}) collective-permute-start(bf16[128,1024]{1,0:T(8,128)(2,1)S(1)} %get-tuple-element.316), channel_id=1, source_target_pairs={{0,1},{1,2},{2,3},{3,4},{4,5},{5,6},{6,7},{7,8},{8,9},{9,10},{10,1... | collective-permute-start | bytes 786440 | tf_op jit(solution)/shard_map/ppermute | solution.py:18
  59.7 20.3 %collective-permute-start = (bf16[128,1024]{1,0:T(8,128)(2,1)}, bf16[128,1024]{1,0:T(8,128)(2,1)}, u32[]{:S(2)}, u32[]{:S(2)}) collective-permute-start(bf16[128,1024]{1,0:T(8,128)(2,1)} %get-tuple-element.318), channel_id=1, source_target_pairs={{0,1},{1,2},{2,3},{3,4},{4,5},{5,6},{6,7},{7,8},{8,9},{9,10},{10,1... | collective-permute-start | bytes 786440 | tf_op jit(solution)/shard_map/ppermute | solution.py:18
  90.6 20.1 %copy-start.13 = (f32[1,1024]{1,0:T(1,128)S(1)}, f32[1,1024]{1,0:T(1,128)}, u32[]{:S(2)}) copy-start(f32[1,1024]{1,0:T(1,128)} %get-tuple-element.340) | copy-start | bytes 12292
  90.7 20.1 %copy-start.14 = (f32[1,1024]{1,0:T(1,128)S(1)}, f32[1,1024]{1,0:T(1,128)}, u32[]{:S(2)}) copy-start(f32[1,1024]{1,0:T(1,128)} %get-tuple-element.341) | copy-start | bytes 12292
  90.7 20.1 %copy-start.15 = (f32[1,1024]{1,0:T(1,128)S(1)}, f32[1,1024]{1,0:T(1,128)}, u32[]{:S(2)}) copy-start(f32[1,1024]{1,0:T(1,128)} %get-tuple-element.342) | copy-start | bytes 12292
  90.7 20.1 %copy-start.16 = (f32[1,1024]{1,0:T(1,128)S(1)}, f32[1,1024]{1,0:T(1,128)}, u32[]{:S(2)}) copy-start(f32[1,1024]{1,0:T(1,128)} %get-tuple-element.343) | copy-start | bytes 12292
  90.7 20.1 %copy-start.17 = (f32[1,1024]{1,0:T(1,128)S(1)}, f32[1,1024]{1,0:T(1,128)}, u32[]{:S(2)}) copy-start(f32[1,1024]{1,0:T(1,128)} %get-tuple-element.344) | copy-start | bytes 12292
  90.7 20.1 %copy-start.18 = (f32[1,1024]{1,0:T(1,128)S(1)}, f32[1,1024]{1,0:T(1,128)}, u32[]{:S(2)}) copy-start(f32[1,1024]{1,0:T(1,128)} %get-tuple-element.345) | copy-start | bytes 12292
  90.7 20.1 %copy-start.19 = (f32[1,1024]{1,0:T(1,128)S(1)}, f32[1,1024]{1,0:T(1,128)}, u32[]{:S(2)}) copy-start(f32[1,1024]{1,0:T(1,128)} %get-tuple-element.346) | copy-start | bytes 12292
  90.7 20.1 %copy-start.20 = (f32[1,1024]{1,0:T(1,128)S(1)}, f32[1,1024]{1,0:T(1,128)}, u32[]{:S(2)}) copy-start(f32[1,1024]{1,0:T(1,128)} %get-tuple-element.347) | copy-start | bytes 12292
  90.7 20.1 %copy-start.21 = (f32[1,1024]{1,0:T(1,128)S(1)}, f32[1,1024]{1,0:T(1,128)}, u32[]{:S(2)}) copy-start(f32[1,1024]{1,0:T(1,128)} %get-tuple-element.348) | copy-start | bytes 12292
  90.7 20.1 %copy-start.22 = (f32[1,1024]{1,0:T(1,128)S(1)}, f32[1,1024]{1,0:T(1,128)}, u32[]{:S(2)}) copy-start(f32[1,1024]{1,0:T(1,128)} %get-tuple-element.349) | copy-start | bytes 12292
  90.7 20.1 %copy-start.23 = (f32[1,1024]{1,0:T(1,128)S(1)}, f32[1,1024]{1,0:T(1,128)}, u32[]{:S(2)}) copy-start(f32[1,1024]{1,0:T(1,128)} %get-tuple-element.350) | copy-start | bytes 12292
  90.8 20.1 %copy-start.24 = (f32[1,1024]{1,0:T(1,128)S(1)}, f32[1,1024]{1,0:T(1,128)}, u32[]{:S(2)}) copy-start(f32[1,1024]{1,0:T(1,128)} %get-tuple-element.351) | copy-start | bytes 12292
  90.8 20.1 %copy-start.25 = (f32[1,1024]{1,0:T(1,128)S(1)}, f32[1,1024]{1,0:T(1,128)}, u32[]{:S(2)}) copy-start(f32[1,1024]{1,0:T(1,128)} %get-tuple-element.321) | copy-start | bytes 12292
  90.8 20.1 %copy-start.26 = (f32[1,1024]{1,0:T(1,128)S(1)}, f32[1,1024]{1,0:T(1,128)}, u32[]{:S(2)}) copy-start(f32[1,1024]{1,0:T(1,128)} %get-tuple-element.322) | copy-start | bytes 12292
  90.8 20.1 %copy-start.27 = (f32[1,1024]{1,0:T(1,128)S(1)}, f32[1,1024]{1,0:T(1,128)}, u32[]{:S(2)}) copy-start(f32[1,1024]{1,0:T(1,128)} %get-tuple-element.323) | copy-start | bytes 12292
  90.8 20.1 %copy-start.28 = (f32[1,1024]{1,0:T(1,128)S(1)}, f32[1,1024]{1,0:T(1,128)}, u32[]{:S(2)}) copy-start(f32[1,1024]{1,0:T(1,128)} %get-tuple-element.324) | copy-start | bytes 12292
  90.8 20.1 %copy-start.29 = (f32[1,1024]{1,0:T(1,128)S(1)}, f32[1,1024]{1,0:T(1,128)}, u32[]{:S(2)}) copy-start(f32[1,1024]{1,0:T(1,128)} %get-tuple-element.325) | copy-start | bytes 12292
  90.8 20.1 %copy-start.30 = (f32[1,1024]{1,0:T(1,128)S(1)}, f32[1,1024]{1,0:T(1,128)}, u32[]{:S(2)}) copy-start(f32[1,1024]{1,0:T(1,128)} %get-tuple-element.326) | copy-start | bytes 12292
  90.8 20.1 %copy-start.31 = (f32[1,1024]{1,0:T(1,128)S(1)}, f32[1,1024]{1,0:T(1,128)}, u32[]{:S(2)}) copy-start(f32[1,1024]{1,0:T(1,128)} %get-tuple-element.327) | copy-start | bytes 12292
  90.8 20.1 %copy-start.32 = (f32[1,1024]{1,0:T(1,128)S(1)}, f32[1,1024]{1,0:T(1,128)}, u32[]{:S(2)}) copy-start(f32[1,1024]{1,0:T(1,128)} %get-tuple-element.328) | copy-start | bytes 12292
  90.8 20.1 %copy-start.33 = (f32[1,1024]{1,0:T(1,128)S(1)}, f32[1,1024]{1,0:T(1,128)}, u32[]{:S(2)}) copy-start(f32[1,1024]{1,0:T(1,128)} %get-tuple-element.329) | copy-start | bytes 12292
  94.3 16.3 %collective-permute-start.2 = (bf16[30,1024]{1,0:T(8,128)(2,1)S(1)}, bf16[30,1024]{1,0:T(8,128)(2,1)S(1)}, u32[]{:S(2)}, u32[]{:S(2)}) collective-permute-start(bf16[30,1024]{1,0:T(8,128)(2,1)S(1)} %slice.294), channel_id=1, source_target_pairs={{0,1},{1,2},{2,3},{3,4},{4,5},{5,6},{6,7},{7,8},{8,9},{9,10},{10,1... | collective-permute-start | bytes 184328 | tf_op jit(solution)/shard_map/ppermute | solution.py:18
  113.6 245.4 %copy-start.7 = (bf16[128,1024]{1,0:T(8,128)(2,1)}, bf16[128,1024]{1,0:T(8,128)(2,1)S(1)}, u32[]{:S(2)}) copy-start(bf16[128,1024]{1,0:T(8,128)(2,1)S(1)} %fusion.23) | copy-start | bytes 786436
  150.6 208.4 %copy-start.10 = (f32[8192]{0:T(1024)S(1)}, f32[8192]{0:T(1024)}, u32[]{:S(2)}) copy-start(f32[8192]{0:T(1024)} %param.28) | copy-start | bytes 98308
  (25 other events, 295.1 us)
Sparse Core Ops, SparseCore 0:
  9.9 39.4 all-gather.5
  50.9 299.7 all-gather.7
  352.7 34.2 all-gather.9
  388.7 37.3 all-gather.13
  427.8 160.7 all-gather.11
where the time goes:
time: 646 us; the launch traced here: 645 us
  waiting for transfers between devices  458 us (71%)
  blocking collectives  59.4 us (9%)
  matrix products  58.1 us (9%)
  starting transfers between devices  20.9 us (3%)
  other arithmetic  18.1 us (3%)
  local copies, waits for them, and re-layouts  15.7 us (2%)
  between operations  14.7 us (2%)
    all_gather x1, waiting for transfers between devices, on_device(): adapter_full = lax.all_gather(adapter_part, 'mp', axis=1, tiled=True)  200 us
    all_gather x1, waiting for transfers between devices, on_device(): lax.all_gather(w_query, 'tm', axis=0, tiled=True)  149 us
    all_gather x1, waiting for transfers between devices, on_device(): adapter_part = lax.all_gather(w_adapter, 'tm', axis=0, tiled=True)  41.4 us
    all_gather x1, blocking collectives, on_device(): shard_pooled = lax.all_gather(pooled, 'mp', axis=0, tiled=True)  36.5 us
    all_gather x1, waiting for transfers between devices, on_device(): lax.all_gather(w_key, 'tm', axis=0, tiled=True)  27.4 us
    all_gather x1, waiting for transfers between devices, on_device(): lax.all_gather(w_value, 'tm', axis=0, tiled=True)  23.5 us
    ppermute x3, starting transfers between devices, passed_along(): return lax.ppermute(value, axis, pairs)  20.7 us
    ppermute x3, waiting for transfers between devices, passed_along(): return lax.ppermute(value, axis, pairs)  14.1 us
  transfers between devices with their start and end apart: 8, of which 8 were waited for; matrix products, arithmetic and copies ran while one was open for 7% of the time, Pallas kernels for 0%

commit v1 on v0

--- a/solution.py
+++ b/solution.py
@@ -10,6 +10,23 @@
 eps_llm = 1e-06
 rope_base = 1000000.0
 masked_score = -1e30
+
+
+def joined_along(parts, dim):
+    lengths = list(parts.shape[1:])
+    lengths[dim] *= parts.shape[0]
+    return jnp.moveaxis(parts, 0, dim).reshape(lengths)
+
+
+def doubled(x, axis):
+    size, index = (lax.axis_size(axis), lax.axis_index(axis))
+    blocks, bit = (x[None], 1)
+    while bit < size:
+        theirs = lax.ppermute(blocks, axis, [(i, i ^ bit) for i in range(size)])
+        low = index & bit == 0
+        blocks = jnp.concatenate([jnp.where(low, blocks, theirs), jnp.where(low, theirs, blocks)])
+        bit *= 2
+    return blocks
 
 
 def passed_along(value, axis, by):
@@ -129,7 +146,7 @@
     ).astype(jnp.bfloat16)
     shard_pooled = lax.all_gather(pooled, "mp", axis=0, tiled=True)
     shard_tokens = shard_pooled.shape[0]
-    adapter_part = lax.all_gather(w_adapter, "tm", axis=0, tiled=True)
+    adapter_part = joined_along(doubled(w_adapter, "tm"), 0)
     adapter_full = lax.all_gather(adapter_part, "mp", axis=1, tiled=True)
     adapted = jnp.dot(shard_pooled, adapter_full, preferred_element_type=jnp.float32)
     llm_in = (

time: 646 us -> 690 us (1.068)
  waiting for transfers between devices: 458 us -> 486 us
  other arithmetic: 18.1 us -> 26.9 us
    ppermute x0 -> x3, waiting for transfers between devices: none -> 71 us  [doubled(): theirs = lax.ppermute(blocks, axis, [(i, i ^ bit) for i in range(size)])]
    all_gather x1 -> x0, waiting for transfers between devices: 41.4 us -> none  [on_device(): adapter_part = lax.all_gather(w_adapter, 'tm', axis=0, tiled=True)]
  transfers between devices with their start and end apart: 8 -> 10, of which waited for: 8 -> 10; matrix products, arithmetic and copies ran while one was open for 7% -> 6% of each run, Pallas kernels for 0% -> 0%
where the time goes in v1:
time: 690 us; the launch traced here: 689 us
  waiting for transfers between devices  486 us (70%)
  blocking collectives  60.1 us (9%)
  matrix products  58.1 us (8%)
  other arithmetic  26.9 us (4%)
  starting transfers between devices  26.3 us (4%)
  local copies, waits for them, and re-layouts  17.6 us (3%)
  between operations  14.7 us (2%)
    all_gather x1, waiting for transfers between devices, on_device(): adapter_full = lax.all_gather(adapter_part, 'mp', axis=1, tiled=True)  201 us
    all_gather x1, waiting for transfers between devices, on_device(): lax.all_gather(w_query, 'tm', axis=0, tiled=True)  149 us
    ppermute x3, waiting for transfers between devices, doubled(): theirs = lax.ppermute(blocks, axis, [(i, i ^ bit) for i in range(size)])  71 us
    all_gather x1, blocking collectives, on_device(): shard_pooled = lax.all_gather(pooled, 'mp', axis=0, tiled=True)  37.3 us
    all_gather x1, waiting for transfers between devices, on_device(): lax.all_gather(w_key, 'tm', axis=0, tiled=True)  27.1 us
    all_gather x1, waiting for transfers between devices, on_device(): lax.all_gather(w_value, 'tm', axis=0, tiled=True)  23.7 us
    ppermute x3, starting transfers between devices, passed_along(): return lax.ppermute(value, axis, pairs)  21 us
  transfers between devices with their start and end apart: 10, of which 10 were waited for; matrix products, arithmetic and copies ran while one was open for 6% of the time, Pallas kernels for 0%

profile of v1, /device:TPU:0, one launch (start us, length us, event | category | flops | bytes accessed | tf_op | source)
XLA Modules:
  0.0 689.5 jit_solution(9937296401977920123)
XLA Ops:
  11.6 2.9 collective-permute-start.4
  14.4 23.6 %collective-permute-done.4 = bf16[2,128,2048]{2,1,0:T(8,128)(2,1)} collective-permute-done((bf16[2,128,2048]{2,1,0:T(8,128)(2,1)S(1)}, bf16[2,128,2048]{2,1,0:T(8,128)(2,1)}, u32[]{:S(2)}, u32[]{:S(2)}) %collective-permute-start.4) | collective-permute-done | bytes 1048608 | tf_op jit(solution)/shard_map/ppermute | solution.py:25
  44.0 45.7 %collective-permute-done.5 = bf16[4,128,2048]{2,1,0:T(8,128)(2,1)} collective-permute-done((bf16[4,128,2048]{2,1,0:T(8,128)(2,1)}, bf16[4,128,2048]{2,1,0:T(8,128)(2,1)}, u32[]{:S(2)}, u32[]{:S(2)}) %collective-permute-start.5) | collective-permute-done | bytes 2097184 | tf_op jit(solution)/shard_map/ppermute | solution.py:25
  96.6 3.9 convolution_convert_fusion
  101.3 3.4 collective-permute-start.1
  104.7 4.2 collective-permute-start
  114.4 8.9 %collective-permute-done = bf16[128,1024]{1,0:T(8,128)(2,1)} collective-permute-done((bf16[128,1024]{1,0:T(8,128)(2,1)}, bf16[128,1024]{1,0:T(8,128)(2,1)}, u32[]{:S(2)}, u32[]{:S(2)}) %collective-permute-start) | collective-permute-done | bytes 262176 | tf_op jit(solution)/shard_map/ppermute | solution.py:35
  129.3 3.8 fusion.22
  134.2 3.2 fusion.72
  137.6 13.4 %collective-permute-start.2 = (bf16[30,1024]{1,0:T(8,128)(2,1)S(1)}, bf16[30,1024]{1,0:T(8,128)(2,1)S(1)}, u32[]{:S(2)}, u32[]{:S(2)}) collective-permute-start(bf16[30,1024]{1,0:T(8,128)(2,1)S(1)} %slice.294), channel_id=1, source_target_pairs={{0,1},{1,2},{2,3},{3,4},{4,5},{5,6},{6,7},{7,8},{8,9},{9,10},{10,1... | collective-permute-start | bytes 184328 | tf_op jit(solution)/shard_map/ppermute | solution.py:35
  151.1 3.0 collective-permute-done.2
  154.5 2.5 fusion.23
  157.5 37.3 %all_gather.21 = bf16[128,1024]{1,0:T(8,128)(2,1)S(1)} all-gather(bf16[32,1024]{1,0:T(8,128)(2,1)S(1)} %multiply_convert_fusion.5), channel_id=1, replica_groups=mesh['tm'=8,'mp'=4] {'mp'}, dimensions={0}, use_global_device_ids=true | all-gather | bytes 327680 | tf_op jit(solution)/shard_map/all_gather | solution.py:147
  194.8 200.7 %all-gather.5.cloned.1.call-done = bf16[1024,8192]{1,0:T(8,128)(2,1)} async-done(((bf16[1024,2048]{1,0:T(8,128)(2,1)}), bf16[1024,8192]{1,0:T(8,128)(2,1)}) %all-gather.5.cloned.1.call-update) | async-done | bytes 16777232 | tf_op jit(solution)/shard_map/all_gather | solution.py:150
  395.6 8.3 %multiply_reduce_fusion = (f32[128]{0:T(128)S(1)}, f32[128,8192]{1,0:T(8,128)S(1)}) fusion(bf16[128,1024]{1,0:T(8,128)(2,1)S(1)} %all_gather.21, bf16[1024,8192]{1,0:T(8,128)(2,1)} %all-gather.5.cloned.1.call-done), kind=kOutput, calls=%fused_computation.36 | convolution fusion | flops 2149580800 | bytes 21234176 | tf_op jit(solution)/shard_map/dot_general | solution.py:151
  404.4 27.1 %all-gather.7.cloned.1.call-done = bf16[8192,256]{1,0:T(8,128)(2,1)} async-done(((bf16[1024,256]{1,0:T(8,128)(2,1)}), bf16[8192,256]{1,0:T(8,128)(2,1)}) %all-gather.7.cloned.1.call-update) | async-done | bytes 4194320 | tf_op jit(solution)/shard_map/all_gather | solution.py:165
  431.5 2.9 fusion.98
  435.0 12.0 %all_gather.24 = bf16[1024,256]{1,0:T(8,128)(2,1)} all-gather(bf16[128,256]{1,0:T(8,128)(2,1)S(1)} %fusion.82), channel_id=1, replica_groups=mesh['tm'=8,'mp'=4] {'tm'}, dimensions={0}, use_global_device_ids=true | all-gather | bytes 589824 | tf_op jit(solution)/shard_map/all_gather | solution.py:193
  447.0 23.7 %all-gather.11.cloned.1.call-done = bf16[8192,256]{1,0:T(8,128)(2,1)} async-done(((bf16[1024,256]{1,0:T(8,128)(2,1)}), bf16[8192,256]{1,0:T(8,128)(2,1)}) %all-gather.11.cloned.1.call-update) | async-done | bytes 4194320 | tf_op jit(solution)/shard_map/all_gather | solution.py:169
  470.7 2.9 convolution_convert_fusion.1
  473.6 10.8 %all_gather.27 = bf16[1024,256]{1,0:T(8,128)(2,1)} all-gather(bf16[128,256]{1,0:T(8,128)(2,1)S(1)} %convolution_convert_fusion.1), channel_id=1, replica_groups=mesh['tm'=8,'mp'=4] {'tm'}, dimensions={0}, use_global_device_ids=true | all-gather | bytes 589824 | tf_op jit(solution)/shard_map/all_gather | solution.py:194
  484.4 148.9 %all-gather.9.cloned.1.call-done = bf16[8192,2048]{1,0:T(8,128)(2,1)} async-done(((bf16[1024,2048]{1,0:T(8,128)(2,1)}), bf16[8192,2048]{1,0:T(8,128)(2,1)}) %all-gather.9.cloned.1.call-update) | async-done | bytes 33554448 | tf_op jit(solution)/shard_map/all_gather | solution.py:161
  633.3 12.9 %fusion.99 = f32[128,2048]{1,0:T(8,128)S(1)} fusion(bf16[128,8192]{1,0:T(8,128)(2,1)S(1)} %multiply_convert_fusion, bf16[8192,2048]{1,0:T(8,128)(2,1)} %all-gather.9.cloned.1.call-done), kind=kOutput, calls=%fused_computation.208 | convolution fusion | flops 4294967296 | bytes 36700160 | tf_op jit(solution)/shard_map/dot_general | solution.py:159
  647.6 2.4 copy.57
  650.0 2.4 copy.58
  654.8 25.1 %while.20 = (s32[]{:T(128)}, f32[2,8,128]{2,1,0:T(8,128)S(1)}, f32[2,8,128]{2,1,0:T(8,128)S(1)}, f32[2,8,128,128]{3,2,1,0:T(8,128)}, s32[8]{0:T(128)S(1)}, /*ind...) while((s32[]{:T(128)}, f32[2,8,128]{2,1,0:T(8,128)S(1)}, ...), condition=%wide.region_14.15_spmd.clone, body=%wide.region_10.14_spmd.clone.sunk | while | flops 551591552 | bytes 26622240 | solution.py:230
  656.4 2.8 fusion.133
  659.2 3.2 fusion.134
  662.5 3.9 fusion.136
  668.9 2.8 fusion.133
  671.7 3.2 fusion.134
  675.0 3.9 fusion.136
  (199 shorter events, 44.2 us)
Async XLA Ops:
  7.2 125.9 %copy-start = (bf16[1024,1024]{1,0:T(8,128)(2,1)S(1)}, bf16[1024,1024]{1,0:T(8,128)(2,1)}, u32[]{:S(2)}) copy-start(bf16[1024,1024]{1,0:T(8,128)(2,1)} %param.22) | copy-start | bytes 6291460
  7.2 388.4 %all-gather.5.cloned.1.call-start = ((), (), s32[]{:S(2)}) async-start(), calls=%async_computation | async-start | bytes 20971520 | tf_op jit(solution)/shard_map/all_gather | solution.py:150
  7.2 2.3 collective-permute-start.3
  11.6 26.4 %collective-permute-start.4 = (bf16[2,128,2048]{2,1,0:T(8,128)(2,1)S(1)}, bf16[2,128,2048]{2,1,0:T(8,128)(2,1)}, u32[]{:S(2)}, u32[]{:S(2)}) collective-permute-start(bf16[2,128,2048]{2,1,0:T(8,128)(2,1)S(1)} %pad_maximum_fusion.2), channel_id=1, source_target_pairs={{0,8},{4,12},{8,0},{12,4},{16,24},{20,28},{24,16},{28,20},{1,9},{5... | collective-permute-start | bytes 3145736 | tf_op jit(solution)/shard_map/ppermute | solution.py:25
  42.2 47.5 %collective-permute-start.5 = (bf16[4,128,2048]{2,1,0:T(8,128)(2,1)}, bf16[4,128,2048]{2,1,0:T(8,128)(2,1)}, u32[]{:S(2)}, u32[]{:S(2)}) collective-permute-start(bf16[4,128,2048]{2,1,0:T(8,128)(2,1)} %pad_maximum_fusion.1), channel_id=1, source_target_pairs={{0,16},{4,20},{8,24},{12,28},{16,0},{20,4},{24,8},{28,12},{1,17},{... | collective-permute-start | bytes 6291464 | tf_op jit(solution)/shard_map/ppermute | solution.py:25
  94.2 337.3 %all-gather.7.cloned.1.call-start = ((), (), s32[]{:S(2)}) async-start(), calls=%async_computation.1 | async-start | bytes 4718592 | tf_op jit(solution)/shard_map/all_gather | solution.py:165
  94.9 375.8 %all-gather.11.cloned.1.call-start = ((), (), s32[]{:S(2)}) async-start(), calls=%async_computation.3 | async-start | bytes 4718592 | tf_op jit(solution)/shard_map/all_gather | solution.py:169
  95.7 537.6 %all-gather.9.cloned.1.call-start = ((), (), s32[]{:S(2)}) async-start(), calls=%async_computation.2 | async-start | bytes 37748736 | tf_op jit(solution)/shard_map/all_gather | solution.py:161
  101.3 12.9 %collective-permute-start.1 = (bf16[128,1024]{1,0:T(8,128)(2,1)S(1)}, bf16[128,1024]{1,0:T(8,128)(2,1)S(1)}, u32[]{:S(2)}, u32[]{:S(2)}) collective-permute-start(bf16[128,1024]{1,0:T(8,128)(2,1)S(1)} %get-tuple-element.322), channel_id=1, source_target_pairs={{0,1},{1,2},{2,3},{3,4},{4,5},{5,6},{6,7},{7,8},{8,9},{9,10},{10,1... | collective-permute-start | bytes 786440 | tf_op jit(solution)/shard_map/ppermute | solution.py:35
  104.7 18.6 %collective-permute-start = (bf16[128,1024]{1,0:T(8,128)(2,1)}, bf16[128,1024]{1,0:T(8,128)(2,1)}, u32[]{:S(2)}, u32[]{:S(2)}) collective-permute-start(bf16[128,1024]{1,0:T(8,128)(2,1)} %get-tuple-element.324), channel_id=1, source_target_pairs={{0,1},{1,2},{2,3},{3,4},{4,5},{5,6},{6,7},{7,8},{8,9},{9,10},{10,1... | collective-permute-start | bytes 786440 | tf_op jit(solution)/shard_map/ppermute | solution.py:35
  133.9 20.3 %copy-start.16 = (f32[1,1024]{1,0:T(1,128)S(1)}, f32[1,1024]{1,0:T(1,128)}, u32[]{:S(2)}) copy-start(f32[1,1024]{1,0:T(1,128)} %get-tuple-element.346) | copy-start | bytes 12292
  133.9 20.3 %copy-start.17 = (f32[1,1024]{1,0:T(1,128)S(1)}, f32[1,1024]{1,0:T(1,128)}, u32[]{:S(2)}) copy-start(f32[1,1024]{1,0:T(1,128)} %get-tuple-element.347) | copy-start | bytes 12292
  133.9 20.3 %copy-start.18 = (f32[1,1024]{1,0:T(1,128)S(1)}, f32[1,1024]{1,0:T(1,128)}, u32[]{:S(2)}) copy-start(f32[1,1024]{1,0:T(1,128)} %get-tuple-element.348) | copy-start | bytes 12292
  133.9 20.3 %copy-start.19 = (f32[1,1024]{1,0:T(1,128)S(1)}, f32[1,1024]{1,0:T(1,128)}, u32[]{:S(2)}) copy-start(f32[1,1024]{1,0:T(1,128)} %get-tuple-element.349) | copy-start | bytes 12292
  133.9 20.3 %copy-start.20 = (f32[1,1024]{1,0:T(1,128)S(1)}, f32[1,1024]{1,0:T(1,128)}, u32[]{:S(2)}) copy-start(f32[1,1024]{1,0:T(1,128)} %get-tuple-element.350) | copy-start | bytes 12292
  133.9 20.3 %copy-start.21 = (f32[1,1024]{1,0:T(1,128)S(1)}, f32[1,1024]{1,0:T(1,128)}, u32[]{:S(2)}) copy-start(f32[1,1024]{1,0:T(1,128)} %get-tuple-element.351) | copy-start | bytes 12292
  134.0 20.3 %copy-start.22 = (f32[1,1024]{1,0:T(1,128)S(1)}, f32[1,1024]{1,0:T(1,128)}, u32[]{:S(2)}) copy-start(f32[1,1024]{1,0:T(1,128)} %get-tuple-element.352) | copy-start | bytes 12292
  134.0 20.3 %copy-start.23 = (f32[1,1024]{1,0:T(1,128)S(1)}, f32[1,1024]{1,0:T(1,128)}, u32[]{:S(2)}) copy-start(f32[1,1024]{1,0:T(1,128)} %get-tuple-element.353) | copy-start | bytes 12292
  134.0 20.3 %copy-start.24 = (f32[1,1024]{1,0:T(1,128)S(1)}, f32[1,1024]{1,0:T(1,128)}, u32[]{:S(2)}) copy-start(f32[1,1024]{1,0:T(1,128)} %get-tuple-element.354) | copy-start | bytes 12292
  134.0 20.3 %copy-start.25 = (f32[1,1024]{1,0:T(1,128)S(1)}, f32[1,1024]{1,0:T(1,128)}, u32[]{:S(2)}) copy-start(f32[1,1024]{1,0:T(1,128)} %get-tuple-element.355) | copy-start | bytes 12292
  134.0 20.3 %copy-start.26 = (f32[1,1024]{1,0:T(1,128)S(1)}, f32[1,1024]{1,0:T(1,128)}, u32[]{:S(2)}) copy-start(f32[1,1024]{1,0:T(1,128)} %get-tuple-element.356) | copy-start | bytes 12292
  134.0 20.3 %copy-start.27 = (f32[1,1024]{1,0:T(1,128)S(1)}, f32[1,1024]{1,0:T(1,128)}, u32[]{:S(2)}) copy-start(f32[1,1024]{1,0:T(1,128)} %get-tuple-element.357) | copy-start | bytes 12292
  134.0 20.3 %copy-start.28 = (f32[1,1024]{1,0:T(1,128)S(1)}, f32[1,1024]{1,0:T(1,128)}, u32[]{:S(2)}) copy-start(f32[1,1024]{1,0:T(1,128)} %get-tuple-element.327) | copy-start | bytes 12292
  134.0 20.3 %copy-start.29 = (f32[1,1024]{1,0:T(1,128)S(1)}, f32[1,1024]{1,0:T(1,128)}, u32[]{:S(2)}) copy-start(f32[1,1024]{1,0:T(1,128)} %get-tuple-element.328) | copy-start | bytes 12292
  134.0 20.3 %copy-start.30 = (f32[1,1024]{1,0:T(1,128)S(1)}, f32[1,1024]{1,0:T(1,128)}, u32[]{:S(2)}) copy-start(f32[1,1024]{1,0:T(1,128)} %get-tuple-element.329) | copy-start | bytes 12292
  134.0 20.3 %copy-start.31 = (f32[1,1024]{1,0:T(1,128)S(1)}, f32[1,1024]{1,0:T(1,128)}, u32[]{:S(2)}) copy-start(f32[1,1024]{1,0:T(1,128)} %get-tuple-element.330) | copy-start | bytes 12292
  134.1 20.3 %copy-start.32 = (f32[1,1024]{1,0:T(1,128)S(1)}, f32[1,1024]{1,0:T(1,128)}, u32[]{:S(2)}) copy-start(f32[1,1024]{1,0:T(1,128)} %get-tuple-element.331) | copy-start | bytes 12292
  134.1 20.3 %copy-start.33 = (f32[1,1024]{1,0:T(1,128)S(1)}, f32[1,1024]{1,0:T(1,128)}, u32[]{:S(2)}) copy-start(f32[1,1024]{1,0:T(1,128)} %get-tuple-element.332) | copy-start | bytes 12292
  134.1 20.3 %copy-start.34 = (f32[1,1024]{1,0:T(1,128)S(1)}, f32[1,1024]{1,0:T(1,128)}, u32[]{:S(2)}) copy-start(f32[1,1024]{1,0:T(1,128)} %get-tuple-element.333) | copy-start | bytes 12292
  137.6 16.5 %collective-permute-start.2 = (bf16[30,1024]{1,0:T(8,128)(2,1)S(1)}, bf16[30,1024]{1,0:T(8,128)(2,1)S(1)}, u32[]{:S(2)}, u32[]{:S(2)}) collective-permute-start(bf16[30,1024]{1,0:T(8,128)(2,1)S(1)} %slice.294), channel_id=1, source_target_pairs={{0,1},{1,2},{2,3},{3,4},{4,5},{5,6},{6,7},{7,8},{8,9},{9,10},{10,1... | collective-permute-start | bytes 184328 | tf_op jit(solution)/shard_map/ppermute | solution.py:35
  157.0 246.8 %copy-start.10 = (bf16[128,1024]{1,0:T(8,128)(2,1)}, bf16[128,1024]{1,0:T(8,128)(2,1)S(1)}, u32[]{:S(2)}) copy-start(bf16[128,1024]{1,0:T(8,128)(2,1)S(1)} %fusion.23) | copy-start | bytes 786436
  194.8 209.0 %copy-start.13 = (f32[8192]{0:T(1024)S(1)}, f32[8192]{0:T(1024)}, u32[]{:S(2)}) copy-start(f32[8192]{0:T(1024)} %param.28) | copy-start | bytes 98308
  (30 other events, 341.0 us)
Sparse Core Ops, SparseCore 0:
  94.3 301.2 all-gather.4
  397.5 33.9 all-gather.6
  433.4 37.2 all-gather.10
  472.4 160.7 all-gather.8
